TPU v7x, 256 devices: a whole 4x4x8 slice. The times are simulated.
256 devices in a mesh: ctx: 64 (over z, x, core), head: 4 (over y).
Axes of the slice: x: 4, y: 4, z: 8, core: 2. Of those that a mesh axis runs over, the one named last changes fastest.
Arguments:
- asking_vectors: bfloat16 [32768, 2048], P('ctx', 'head'), may hold values from -6 to 6
- lookup_vectors: bfloat16 [32768, 2048], P('ctx', 'head'), may hold values from -16 to 16
- payload_vectors: bfloat16 [32768, 2048], P('ctx', 'head'), may hold values from -16 to 16
- segment_owner_ids: int32 [128], P('ctx'), may hold values from 0 to 31, never falling along the last dimension, each value on 1 to 12 neighbouring positions
- attender_logit_factor: float32 [16], P('head'), may hold values from 4 to 16
- tier_logit_shift: float32 [16], P('head'), may hold values from -0.2 to 0.4
- final_projection_weights: bfloat16 [2048, 4096], P('head'), may hold values from -0.125 to 0.125
Outputs:
- mixed: bfloat16 [32768, 4096], P('ctx', 'head')
All inputs are finite; a program needn't handle non-finite values.
Results may differ from a plain program's by a relative error of at most 0.011.
Values may be sent and summed in bfloat16 or wider, within the bound.
No kernel may reach another device: no remote copies, remote signals or barrier semaphores. Data moves between devices by JAX's collectives and lax.ppermute only.
A program may use at most 64 MiB of HBM per device.

v0:
```python
import functools
import math

import jax
import jax.numpy as jnp
from jax import lax
from jax.experimental import pallas as pl
from jax.experimental.pallas import tpu as pltpu
from jax.sharding import PartitionSpec as P


EPS = 1e-06
HD = 128
LOG2E = math.log2(math.e)
F32 = jnp.float32
BF16 = jnp.bfloat16
GRANT = 12 << 20
PREP_GRANT = 50 << 20
TURNS = (1, 3, 2)
VM = pl.BlockSpec(memory_space=pltpu.VMEM)
HB = pl.BlockSpec(memory_space=pltpu.HBM)
SM = pl.BlockSpec(memory_space=pltpu.SMEM)


def flip(block, mask):
    count = lax.axis_size("ctx")
    return lax.ppermute(block, "ctx", [(i, i ^ mask) for i in range(count)])


def turn(block, shift):
    count = lax.axis_size("head")
    return lax.ppermute(block, "head", [(i, (i + shift) % count) for i in range(count)])


def call(body, outs, specs, scratch=(), flops=0, grant=GRANT):
    return pl.pallas_call(
        body,
        out_shape=outs,
        in_specs=specs,
        out_specs=jax.tree.map(lambda _: VM, outs),
        scratch_shapes=scratch,
        cost_estimate=pl.CostEstimate(flops=flops, bytes_accessed=1 << 20, transcendentals=0),
        compiler_params=pltpu.CompilerParams(vmem_limit_bytes=grant),
    )


def unit(x):
    return x * lax.rsqrt(jnp.mean(x * x, axis=-1, keepdims=True) + EPS)


def prep_body(
    k_hbm, v_hbm, w_hbm, near_ref, v_ref, one_ref, two_ref, three_ref, far_ref, o1, o2, o3,
    kbuf, buf, ksem, vsem, wsem, *, heads,
):
    rows = kbuf.shape[0]
    part = o1.shape[1]
    count = lax.axis_size("head")
    y = lax.axis_index("head")
    c = lax.axis_index("ctx") % 2
    ks, vs, ws = [], [], []
    for h in range(heads):
        cols = slice(h * HD, (h + 1) * HD)
        ks.append(pltpu.make_async_copy(k_hbm.at[:, cols], kbuf.at[:, cols], ksem.at[h]))
        vs.append(pltpu.make_async_copy(v_hbm.at[:, cols], v_ref.at[:, cols], vsem.at[h]))
    for i, (s, out) in enumerate(zip(TURNS, (o1, o2, o3))):
        at = pl.ds(pl.multiple_of((((y + s) % count) * 2 + c) * part, 128), part)
        ws.append(pltpu.make_async_copy(w_hbm.at[:, at], out, wsem.at[i]))
    for h in range(heads):
        ks[h].start()
        vs[h].start()
    for copy in ws:
        copy.start()
    for h in range(heads):
        cols = slice(h * HD, (h + 1) * HD)
        for piece in range(2):
            if piece == 0:
                ks[h].wait()
                x = unit(kbuf[:, cols].astype(F32))
                near_ref[:, cols] = x.astype(BF16)
            else:
                vs[h].wait()
                x = v_ref[:, cols].astype(F32)
            buf[h, piece, 0:rows, :] = x
            n = rows
            scale = 1.0
            at = 0
            for level in range(1, 7):
                n = n // 2
                scale = scale * 0.5
                x = buf[h, piece, pl.ds(0, n, 2), :] + buf[h, piece, pl.ds(1, n, 2), :]
                out = (x * scale).astype(BF16)
                if level == 1:
                    one_ref[piece, :, cols] = out
                elif level == 2:
                    two_ref[piece, :, cols] = out
                elif level == 3:
                    three_ref[piece, :, cols] = out
                else:
                    far_ref[piece, at : at + n, cols] = out
                    at += n
                if level < 6:
                    buf[h, piece, 0:n, :] = x
    for copy in ws:
        copy.wait()


def mixin(qb, pairs):
    acc = None
    for key, val, off in pairs:
        s = lax.dot_general(qb, key, (((1,), (1,)), ((), ())), preferred_element_type=F32)
        if off is not None:
            s = s + off
        p = jnp.exp2(s).astype(BF16)
        aug = jnp.concatenate([val, jnp.ones_like(val)], axis=1)
        o = jnp.dot(p, aug, preferred_element_type=F32)
        acc = o if acc is None else acc + o
    return acc


def near_body(own_ref, fac_ref, sh_ref, q_ref, near_ref, v_ref, one_ref, qs_ref, acc_ref, *, heads):
    rows = q_ref.shape[0]
    half = rows // 2
    bias = jnp.where(own_ref[0] == own_ref[1], 0.0, -1e30).astype(F32)
    for h in range(heads):
        cols = slice(h * HD, (h + 1) * HD)
        wide = slice(2 * h * HD, 2 * (h + 1) * HD)
        q = unit(q_ref[:, cols].astype(F32)) * (fac_ref[h] * (LOG2E / HD))
        qs_ref[:, cols] = q.astype(BF16)
        off = sh_ref[h] * -LOG2E
        for b in range(2):
            own = slice(b * half, (b + 1) * half)
            oth = slice((1 - b) * half, (2 - b) * half)
            qb = qs_ref[own, cols]
            acc_ref[own, wide] = mixin(
                qb,
                [
                    (near_ref[own, cols], v_ref[own, cols], None),
                    (near_ref[oth, cols], v_ref[oth, cols], bias),
                    (one_ref[0, :, cols], one_ref[1, :, cols], off),
                ],
            )


def gather(refs, part, lo, n, cols):
    return jnp.concatenate([r[part, lo : lo + n, cols] for r in refs], axis=0)


def join_body(*refs):
    out_ref = refs[-1]
    at = 0
    for ref in refs[:-1]:
        n = ref.shape[1]
        out_ref[:, at : at + n] = ref[...]
        at += n


def mid_body(sh_ref, qs_ref, acc_ref, a_ref, b_ref, out_ref, *, heads):
    both = (a_ref, b_ref)
    half = qs_ref.shape[0] // 2
    for h in range(heads):
        cols = slice(h * HD, (h + 1) * HD)
        wide = slice(2 * h * HD, 2 * (h + 1) * HD)
        shift = sh_ref[h] * -LOG2E
        pairs = [
            (gather(both, 0, 128 * f, 128, cols), gather(both, 1, 128 * f, 128, cols), (2.0 + f) * shift)
            for f in range(2)
        ]
        for b in range(2):
            own = slice(b * half, (b + 1) * half)
            out_ref[own, wide] = acc_ref[own, wide] + mixin(qs_ref[own, cols], pairs)


def far_body(sh_ref, qs_ref, acc_ref, *refs, block, heads):
    far, both, out_ref = refs[0:6], refs[6:8], refs[8]
    half = qs_ref.shape[0] // 2
    own = slice(block * half, (block + 1) * half)
    for h in range(heads):
        cols = slice(h * HD, (h + 1) * HD)
        shift = sh_ref[h] * -LOG2E
        pairs = []
        for f in range(3):
            rows = [
                jnp.concatenate([gather(far, p, 32 * f, 32, cols), gather(both, p, 256 + 32 * f, 32, cols)], axis=0)
                for p in range(2)
            ]
            pairs.append((rows[0], rows[1], (4.0 + f) * shift))
        got = mixin(qs_ref[own, cols], pairs)
        num = acc_ref[own, 2 * h * HD : (2 * h + 1) * HD] + got[:, 0:HD]
        den = acc_ref[own, (2 * h + 1) * HD : (2 * h + 2) * HD] + got[:, HD:]
        out_ref[:, cols] = (num / den).astype(BF16)


def own_body(w_ref, a_ref, b_ref, out_ref, buf, sem):
    span = buf.shape[1]
    at = pl.multiple_of(lax.axis_index("head") * span, 128)
    copy = pltpu.make_async_copy(w_ref.at[:, pl.ds(at, span)], buf, sem)
    copy.start()
    copy.wait()
    for i, a in enumerate((a_ref, b_ref)):
        n = a.shape[0]
        out_ref[i * n : (i + 1) * n, :] = jnp.dot(a[...], buf[...], preferred_element_type=F32)


def add_body(acc_ref, *refs, terms):
    blocks, ours, theirs, out_ref = refs[: 2 * terms], refs[2 * terms : 3 * terms], refs[3 * terms : 4 * terms], refs[-1]
    width = ours[0].shape[1]
    c = lax.axis_index("ctx") % 2
    for place, ws in ((c, ours), (1 - c, theirs)):
        at = pl.ds(pl.multiple_of(place * width, 128), width)
        for i in range(2):
            n = blocks[0].shape[0]
            rs = slice(i * n, (i + 1) * n)
            acc = acc_ref[rs, at]
            for t, w in enumerate(ws):
                acc += jnp.dot(blocks[2 * t + i][...], w[...], preferred_element_type=F32)
            out_ref[rs, at] = acc.astype(out_ref.dtype)


def per_device(q, k, v, owner, factor, shift, w):
    rows, wide = q.shape
    heads = factor.shape[0]
    S = jax.ShapeDtypeStruct
    nh = lax.axis_size("head")
    span = w.shape[1] // nh
    part = span // 2
    k_rows = w.shape[0]

    near, v_in, one, two, three, far, *slabs = call(
        functools.partial(prep_body, heads=heads),
        [
            S((rows, wide), BF16),
            S((rows, wide), BF16),
            S((2, 256, wide), BF16),
            S((2, 128, wide), BF16),
            S((2, 64, wide), BF16),
            S((2, 56, wide), BF16),
            *[S((k_rows, part), BF16)] * 3,
        ],
        [HB, HB, HB],
        scratch=[
            pltpu.VMEM((rows, wide), BF16),
            pltpu.VMEM((heads, 2, rows, HD), F32),
            pltpu.SemaphoreType.DMA((heads,)),
            pltpu.SemaphoreType.DMA((heads,)),
            pltpu.SemaphoreType.DMA((3,)),
        ],
        grant=PREP_GRANT,
    )(k, v, w)
    send = [turn(b, s) for b, s in zip(slabs, TURNS)]

    f1 = flip(far, 8)
    one_o = flip(one, 1)
    two_x = flip(two, 2)
    three_x2 = flip(three, 4)
    three_x3 = flip(three, 6)

    m5 = jnp.concatenate([far[:, 32:48], f1[:, 32:48]], axis=1)
    m6 = jnp.concatenate([far[:, 48:56], f1[:, 48:56]], axis=1)
    f2 = flip(m5, 16)
    f3 = [flip(m6, 40), flip(m6, 48)]

    qs, acc = call(
        functools.partial(near_body, heads=heads),
        [S((rows, wide), BF16), S((rows, 2 * wide), F32)],
        [SM, SM, SM, VM, VM, VM, VM],
        flops=1 << 30,
    )(owner, factor, shift, q, near, v_in, one_o)

    mine = jnp.concatenate([f1[:, 0:32], f2, *f3], axis=1)
    far_own = [flip(mine, m) for m in (2, 6, 4)]
    held = call(join_body, S((2, 352, wide), BF16), [VM] * 4)(two_x, three_x2, three_x3, mine)
    held_o = flip(held, 1)
    acc = call(
        functools.partial(mid_body, heads=heads),
        S((rows, 2 * wide), F32),
        [SM] + [VM] * 4,
        flops=1 << 29,
    )(shift, qs, acc, held, held_o)

    far_oth = [flip(b, 1) for b in far_own]
    att = []
    for i in range(2):
        att.append(
            call(
                functools.partial(far_body, block=i, heads=heads),
                S((rows // 2, wide), BF16),
                [SM] + [VM] * 10,
                flops=1 << 28,
            )(shift, qs, acc, *far_own, *far_oth, held, held_o)
        )

    left = [turn(a, 1) for a in att]
    right = [turn(a, 3) for a in att]
    across = [turn(left[0], 1), turn(right[1], 3)]

    w_oth = [flip(b, 1) for b in send]
    out = call(
        own_body,
        S((rows, span), F32),
        [HB, VM, VM],
        scratch=[pltpu.VMEM((k_rows, span), BF16), pltpu.SemaphoreType.DMA],
        flops=1 << 29,
    )(pltpu.with_memory_space_constraint(w, pltpu.HBM), *att)
    out = call(
        functools.partial(add_body, terms=2), S((rows, span), F32), [VM] * 9, flops=1 << 30
    )(out, *left, *right, *send[:2], *w_oth[:2])
    return call(
        functools.partial(add_body, terms=1), S((rows, span), BF16), [VM] * 5, flops=1 << 29
    )(out, *across, send[2], w_oth[2])


def solution(mesh):
    placed = (
        P("ctx", "head"),
        P("ctx", "head"),
        P("ctx", "head"),
        P("ctx"),
        P("head"),
        P("head"),
        P("head", None),
    )

    return jax.shard_map(
        per_device, mesh=mesh, in_specs=placed, out_specs=P("ctx", "head"), check_vma=False
    )
```

profile of v0, /device:TPU:1, one launch (start us, length us, event | category | flops | bytes accessed | tf_op | source)
XLA Modules:
  0.0 92.7 jit_solution(8368271051190686957)
XLA Ops:
  0.0 2.3 %shard_map.73 = (bf16[512,512]{1,0:T(8,128)(2,1)S(1)}, bf16[512,512]{1,0:T(8,128)(2,1)S(1)}, bf16[2,256,512]{2,1,0:T(8,128)(2,1)S(1)}, bf16[2,128,512]{2,1,0:T(8...) custom-call(bf16[512,512]{1,0:T(8,128)(2,1)} %k_hbm.1, ...), custom_call_target="tpu_custom_call" | custom-call | bytes 1048576 | tf_op jit(solution)/shard_map/pallas_call | solution.py:228
  2.3 2.5 %collective-permute-start.4 = (bf16[2,56,512]{2,1,0:T(8,128)(2,1)S(1)}, bf16[2,56,512]{2,1,0:T(8,128)(2,1)S(1)}, u32[]{:S(2)}, u32[]{:S(2)}) collective-permute-start(bf16[2,56,512]{2,1,0:T(8,128)(2,1)S(1)} %get-tuple-element.23), channel_id=1, source_target_pairs={{0,32},{4,36},{8,40},{12,44},{16,48},{20,52},{24,56},{28,60},{32,0... | collective-permute-start | bytes 344072 | tf_op jit(solution)/shard_map/ppermute | solution.py:27
  4.9 2.2 %collective-permute-done.4 = bf16[2,56,512]{2,1,0:T(8,128)(2,1)S(1)} collective-permute-done((bf16[2,56,512]{2,1,0:T(8,128)(2,1)S(1)}, bf16[2,56,512]{2,1,0:T(8,128)(2,1)S(1)}, u32[]{:S(2)}, u32[]{:S(2)}) %collective-permute-start.4) | collective-permute-done | bytes 114720 | tf_op jit(solution)/shard_map/ppermute | solution.py:27
  7.1 3.6 %collective-permute-start.5 = (bf16[2,32,512]{2,1,0:T(8,128)(2,1)S(1)}, bf16[2,32,512]{2,1,0:T(8,128)(2,1)S(1)}, u32[]{:S(2)}, u32[]{:S(2)}) collective-permute-start(bf16[2,32,512]{2,1,0:T(8,128)(2,1)S(1)} %pad_maximum_fusion.1), channel_id=1, source_target_pairs={{0,64},{4,68},{8,72},{12,76},{16,80},{20,84},{24,88},{28,92},{32,9... | collective-permute-start | bytes 196616 | tf_op jit(solution)/shard_map/ppermute | solution.py:27
  10.7 4.3 %collective-permute-start.6 = (bf16[2,16,512]{2,1,0:T(8,128)(2,1)S(1)}, bf16[2,16,512]{2,1,0:T(8,128)(2,1)S(1)}, u32[]{:S(2)}, u32[]{:S(2)}) collective-permute-start(bf16[2,16,512]{2,1,0:T(8,128)(2,1)S(1)} %pad_maximum_fusion.2), channel_id=1, source_target_pairs={{0,160},{4,164},{8,168},{12,172},{16,176},{20,180},{24,184},{28,18... | collective-permute-start | bytes 98312 | tf_op jit(solution)/shard_map/ppermute | solution.py:27
  16.3 2.5 %collective-permute-start.2 = (bf16[2,64,512]{2,1,0:T(8,128)(2,1)S(1)}, bf16[2,64,512]{2,1,0:T(8,128)(2,1)S(1)}, u32[]{:S(2)}, u32[]{:S(2)}) collective-permute-start(bf16[2,64,512]{2,1,0:T(8,128)(2,1)S(1)} %get-tuple-element.22), channel_id=1, source_target_pairs={{0,16},{4,20},{8,24},{12,28},{16,0},{20,4},{24,8},{28,12},{32,48},... | collective-permute-start | bytes 393224 | tf_op jit(solution)/shard_map/ppermute | solution.py:27
  18.7 1.5 %collective-permute-start.3 = (bf16[2,64,512]{2,1,0:T(8,128)(2,1)S(1)}, bf16[2,64,512]{2,1,0:T(8,128)(2,1)S(1)}, u32[]{:S(2)}, u32[]{:S(2)}) collective-permute-start(bf16[2,64,512]{2,1,0:T(8,128)(2,1)S(1)} %get-tuple-element.22), channel_id=1, source_target_pairs={{0,24},{4,28},{8,16},{12,20},{16,8},{20,12},{24,0},{28,4},{32,56},... | collective-permute-start | bytes 393224 | tf_op jit(solution)/shard_map/ppermute | solution.py:27
  21.5 1.8 %collective-permute-start.10 = (bf16[2,96,512]{2,1,0:T(8,128)(2,1)S(1)}, bf16[2,96,512]{2,1,0:T(8,128)(2,1)S(1)}, u32[]{:S(2)}, u32[]{:S(2)}) collective-permute-start(bf16[2,96,512]{2,1,0:T(8,128)(2,1)S(1)} %pad_maximum_fusion.refs_3_), channel_id=1, source_target_pairs={{0,24},{4,28},{8,16},{12,20},{16,8},{20,12},{24,0},{28,4},{32,56},... | collective-permute-start | bytes 589832 | tf_op jit(solution)/shard_map/ppermute | solution.py:27
  23.3 2.2 %collective-permute-done.2.refs_1_ = bf16[2,64,512]{2,1,0:T(8,128)(2,1)S(1)} collective-permute-done((bf16[2,64,512]{2,1,0:T(8,128)(2,1)S(1)}, bf16[2,64,512]{2,1,0:T(8,128)(2,1)S(1)}, u32[]{:S(2)}, u32[]{:S(2)}) %collective-permute-start.2) | collective-permute-done | bytes 131104 | tf_op jit(solution)/shard_map/ppermute | solution.py:27
  26.1 6.3 %collective-permute-start.8 = (bf16[2,352,512]{2,1,0:T(8,128)(2,1)S(1)}, bf16[2,352,512]{2,1,0:T(8,128)(2,1)S(1)}, u32[]{:S(2)}, u32[]{:S(2)}) collective-permute-start(bf16[2,352,512]{2,1,0:T(8,128)(2,1)S(1)} %shard_map.75.a_ref.refs_6_), channel_id=1, source_target_pairs={{0,4},{4,0},{8,12},{12,8},{16,20},{20,16},{24,28},{28,24},{32,36},... | collective-permute-start | bytes 2162696 | tf_op jit(solution)/shard_map/ppermute | solution.py:27
  35.9 2.1 %collective-permute-start.25 = (bf16[512,512]{1,0:T(8,128)(2,1)S(1)}, bf16[512,512]{1,0:T(8,128)(2,1)S(1)}, u32[]{:S(2)}, u32[]{:S(2)}) collective-permute-start(bf16[512,512]{1,0:T(8,128)(2,1)S(1)} %get-tuple-element.26), channel_id=1, source_target_pairs={{0,2},{1,3},{2,0},{3,1},{4,6},{5,7},{6,4},{7,5},{8,10},{9,11},{10,... | collective-permute-start | bytes 1572872 | tf_op jit(solution)/shard_map/ppermute | solution.py:32
  38.1 9.0 %collective-permute-done.19.refs_4_ = bf16[512,512]{1,0:T(8,128)(2,1)S(1)} collective-permute-done((bf16[512,512]{1,0:T(8,128)(2,1)S(1)}, bf16[512,512]{1,0:T(8,128)(2,1)S(1)}, u32[]{:S(2)}, u32[]{:S(2)}) %collective-permute-start.19) | collective-permute-done | bytes 524320 | tf_op jit(solution)/shard_map/ppermute | solution.py:32
  48.8 10.6 %collective-permute-done.25.refs_2_ = bf16[512,512]{1,0:T(8,128)(2,1)S(1)} collective-permute-done((bf16[512,512]{1,0:T(8,128)(2,1)S(1)}, bf16[512,512]{1,0:T(8,128)(2,1)S(1)}, u32[]{:S(2)}, u32[]{:S(2)}) %collective-permute-start.25) | collective-permute-done | bytes 524320 | tf_op jit(solution)/shard_map/ppermute | solution.py:32
  60.4 2.6 %shard_map.74 = (bf16[512,512]{1,0:T(8,128)(2,1)S(1)}, f32[512,1024]{1,0:T(8,128)S(1)}) custom-call(s32[2]{0:T(128)S(1)} %copy-done.2, f32[4]{0:T(128)S(1)} %copy-done.3, f32[4]{0:T(128)S(1)} %copy-done, bf16[512,512]{1,0:T(8,128)(2,1)S(1)} %copy-done.1, bf16[512,512]{1,0:T(8,128)(2,1)S(1)} %get-tuple-element.16.near_ref, ...), custom_call_target="tpu_custom_call" | custom-call | flops 1073741824 | bytes 1048576 | tf_op jit(solution)/shard_map/pallas_call | solution.py:262
  63.0 2.0 %shard_map.76.acc_ref = f32[512,1024]{1,0:T(8,128)S(1)} custom-call(f32[4]{0:T(128)S(1)} %copy-done, bf16[512,512]{1,0:T(8,128)(2,1)S(1)} %get-tuple-element.19.qs_ref, f32[512,1024]{1,0:T(8,128)S(1)} %get-tuple-element.20.acc_ref, bf16[2,352,512]{2,1,0:T(8,128)(2,1)S(1)} %shard_map.75.a_ref.refs_6_, ...), custom_call_target="tpu_custom_call" | custom-call | flops 536870912 | bytes 1048576 | tf_op jit(solution)/shard_map/pallas_call | solution.py:273
  65.6 1.7 %shard_map.78.b_ref = bf16[256,512]{1,0:T(8,128)(2,1)S(1)} custom-call(f32[4]{0:T(128)S(1)} %copy-done, bf16[512,512]{1,0:T(8,128)(2,1)S(1)} %get-tuple-element.19.qs_ref, f32[512,1024]{1,0:T(8,128)S(1)} %shard_map.76.acc_ref, bf16[2,96,512]{2,1,0:T(8,128)(2,1)S(1)} %collective-permute-done.9.refs_0_, ...), custom_call_target="tpu_custom_call" | custom-call | flops 268435456 | bytes 1048576 | tf_op jit(solution)/shard_map/pallas_call | solution.py:284
  67.3 2.1 %collective-permute-start.18 = (bf16[256,512]{1,0:T(8,128)(2,1)S(1)}, bf16[256,512]{1,0:T(8,128)(2,1)S(1)}, u32[]{:S(2)}, u32[]{:S(2)}) collective-permute-start(bf16[256,512]{1,0:T(8,128)(2,1)S(1)} %shard_map.78.b_ref), channel_id=1, source_target_pairs={{0,3},{1,0},{2,1},{3,2},{4,7},{5,4},{6,5},{7,6},{8,11},{9,8},{10,9... | collective-permute-start | bytes 786440 | tf_op jit(solution)/shard_map/ppermute | solution.py:32
  69.4 1.7 %shard_map.77.a_ref = bf16[256,512]{1,0:T(8,128)(2,1)S(1)} custom-call(f32[4]{0:T(128)S(1)} %copy-done, bf16[512,512]{1,0:T(8,128)(2,1)S(1)} %get-tuple-element.19.qs_ref, f32[512,1024]{1,0:T(8,128)S(1)} %shard_map.76.acc_ref, bf16[2,96,512]{2,1,0:T(8,128)(2,1)S(1)} %collective-permute-done.9.refs_0_, ...), custom_call_target="tpu_custom_call" | custom-call | flops 268435456 | bytes 1048576 | tf_op jit(solution)/shard_map/pallas_call | solution.py:284
  71.6 2.5 %collective-permute-start.17 = (bf16[256,512]{1,0:T(8,128)(2,1)S(1)}, bf16[256,512]{1,0:T(8,128)(2,1)S(1)}, u32[]{:S(2)}, u32[]{:S(2)}) collective-permute-start(bf16[256,512]{1,0:T(8,128)(2,1)S(1)} %shard_map.77.a_ref), channel_id=1, source_target_pairs={{0,3},{1,0},{2,1},{3,2},{4,7},{5,4},{6,5},{7,6},{8,11},{9,8},{10,9... | collective-permute-start | bytes 786440 | tf_op jit(solution)/shard_map/ppermute | solution.py:32
  75.3 3.0 %collective-permute-start.24 = (bf16[256,512]{1,0:T(8,128)(2,1)S(1)}, bf16[256,512]{1,0:T(8,128)(2,1)S(1)}, u32[]{:S(2)}, u32[]{:S(2)}) collective-permute-start(bf16[256,512]{1,0:T(8,128)(2,1)S(1)} %collective-permute-done.18.refs_3_), channel_id=1, source_target_pairs={{0,3},{1,0},{2,1},{3,2},{4,7},{5,4},{6,5},{7,6},{8,11},{9,8},{10,9... | collective-permute-start | bytes 786440 | tf_op jit(solution)/shard_map/ppermute | solution.py:32
  79.8 1.9 %shard_map.79.acc_ref = f32[512,1024]{1,0:T(8,128)S(1)} custom-call(bf16[512,4096]{1,0:T(8,128)(2,1)} %w_ref.1, bf16[256,512]{1,0:T(8,128)(2,1)S(1)} %shard_map.77.a_ref, bf16[256,512]{1,0:T(8,128)(2,1)S(1)} %shard_map.78.b_ref), custom_call_target="tpu_custom_call" | custom-call | flops 536870912 | bytes 1048576 | tf_op jit(solution)/shard_map/pallas_call | solution.py:297
  81.7 3.7 %collective-permute-done.16.refs_1_ = bf16[256,512]{1,0:T(8,128)(2,1)S(1)} collective-permute-done((bf16[256,512]{1,0:T(8,128)(2,1)S(1)}, bf16[256,512]{1,0:T(8,128)(2,1)S(1)}, u32[]{:S(2)}, u32[]{:S(2)}) %collective-permute-start.16) | collective-permute-done | bytes 262176 | tf_op jit(solution)/shard_map/ppermute | solution.py:32
  86.7 4.3 %collective-permute-done.23.refs_0_ = bf16[256,512]{1,0:T(8,128)(2,1)S(1)} collective-permute-done((bf16[256,512]{1,0:T(8,128)(2,1)S(1)}, bf16[256,512]{1,0:T(8,128)(2,1)S(1)}, u32[]{:S(2)}, u32[]{:S(2)}) %collective-permute-start.23) | collective-permute-done | bytes 262176 | tf_op jit(solution)/shard_map/ppermute | solution.py:32
  91.0 1.7 %shard_map.81 = bf16[512,1024]{1,0:T(8,128)(2,1)} custom-call(f32[512,1024]{1,0:T(8,128)S(1)} %shard_map.80.acc_ref, bf16[256,512]{1,0:T(8,128)(2,1)S(1)} %collective-permute-done.23.refs_0_, bf16[256,512]{1,0:T(8,128)(2,1)S(1)} %collective-permute-done.24.refs_1_, bf16[512,512]{1,0:T(8,128)(2,1)S(1)} %collective-permute-done.25.refs_2_, ...), custom_call_target="tpu_custom_call" | custom-call | flops 536870912 | bytes 1048576 | tf_op jit(solution)/shard_map/pallas_call | solution.py:307
  (55 shorter events, 14.3 us)
Async XLA Ops:
  7.1 13.2 %collective-permute-start.5 = (bf16[2,32,512]{2,1,0:T(8,128)(2,1)S(1)}, bf16[2,32,512]{2,1,0:T(8,128)(2,1)S(1)}, u32[]{:S(2)}, u32[]{:S(2)}) collective-permute-start(bf16[2,32,512]{2,1,0:T(8,128)(2,1)S(1)} %pad_maximum_fusion.1), channel_id=1, source_target_pairs={{0,64},{4,68},{8,72},{12,76},{16,80},{20,84},{24,88},{28,92},{32,9... | collective-permute-start | bytes 196616 | tf_op jit(solution)/shard_map/ppermute | solution.py:27
  10.7 8.0 %collective-permute-start.6 = (bf16[2,16,512]{2,1,0:T(8,128)(2,1)S(1)}, bf16[2,16,512]{2,1,0:T(8,128)(2,1)S(1)}, u32[]{:S(2)}, u32[]{:S(2)}) collective-permute-start(bf16[2,16,512]{2,1,0:T(8,128)(2,1)S(1)} %pad_maximum_fusion.2), channel_id=1, source_target_pairs={{0,160},{4,164},{8,168},{12,172},{16,176},{20,180},{24,184},{28,18... | collective-permute-start | bytes 98312 | tf_op jit(solution)/shard_map/ppermute | solution.py:27
  15.0 11.0 %collective-permute-start.1 = (bf16[2,128,512]{2,1,0:T(8,128)(2,1)S(1)}, bf16[2,128,512]{2,1,0:T(8,128)(2,1)S(1)}, u32[]{:S(2)}, u32[]{:S(2)}) collective-permute-start(bf16[2,128,512]{2,1,0:T(8,128)(2,1)S(1)} %get-tuple-element.21), channel_id=1, source_target_pairs={{0,8},{4,12},{8,0},{12,4},{16,24},{20,28},{24,16},{28,20},{32,40},... | collective-permute-start | bytes 786440 | tf_op jit(solution)/shard_map/ppermute | solution.py:27
  16.3 9.3 %collective-permute-start.2 = (bf16[2,64,512]{2,1,0:T(8,128)(2,1)S(1)}, bf16[2,64,512]{2,1,0:T(8,128)(2,1)S(1)}, u32[]{:S(2)}, u32[]{:S(2)}) collective-permute-start(bf16[2,64,512]{2,1,0:T(8,128)(2,1)S(1)} %get-tuple-element.22), channel_id=1, source_target_pairs={{0,16},{4,20},{8,24},{12,28},{16,0},{20,4},{24,8},{28,12},{32,48},... | collective-permute-start | bytes 393224 | tf_op jit(solution)/shard_map/ppermute | solution.py:27
  18.7 7.3 %collective-permute-start.3 = (bf16[2,64,512]{2,1,0:T(8,128)(2,1)S(1)}, bf16[2,64,512]{2,1,0:T(8,128)(2,1)S(1)}, u32[]{:S(2)}, u32[]{:S(2)}) collective-permute-start(bf16[2,64,512]{2,1,0:T(8,128)(2,1)S(1)} %get-tuple-element.22), channel_id=1, source_target_pairs={{0,24},{4,28},{8,16},{12,20},{16,8},{20,12},{24,0},{28,4},{32,56},... | collective-permute-start | bytes 393224 | tf_op jit(solution)/shard_map/ppermute | solution.py:27
  20.3 13.4 %collective-permute-start.9 = (bf16[2,96,512]{2,1,0:T(8,128)(2,1)S(1)}, bf16[2,96,512]{2,1,0:T(8,128)(2,1)S(1)}, u32[]{:S(2)}, u32[]{:S(2)}) collective-permute-start(bf16[2,96,512]{2,1,0:T(8,128)(2,1)S(1)} %pad_maximum_fusion.refs_3_), channel_id=1, source_target_pairs={{0,8},{4,12},{8,0},{12,4},{16,24},{20,28},{24,16},{28,20},{32,40},... | collective-permute-start | bytes 589832 | tf_op jit(solution)/shard_map/ppermute | solution.py:27
  21.5 13.6 %collective-permute-start.10 = (bf16[2,96,512]{2,1,0:T(8,128)(2,1)S(1)}, bf16[2,96,512]{2,1,0:T(8,128)(2,1)S(1)}, u32[]{:S(2)}, u32[]{:S(2)}) collective-permute-start(bf16[2,96,512]{2,1,0:T(8,128)(2,1)S(1)} %pad_maximum_fusion.refs_3_), channel_id=1, source_target_pairs={{0,24},{4,28},{8,16},{12,20},{16,8},{20,12},{24,0},{28,4},{32,56},... | collective-permute-start | bytes 589832 | tf_op jit(solution)/shard_map/ppermute | solution.py:27
  25.5 10.4 %collective-permute-start.11 = (bf16[2,96,512]{2,1,0:T(8,128)(2,1)S(1)}, bf16[2,96,512]{2,1,0:T(8,128)(2,1)S(1)}, u32[]{:S(2)}, u32[]{:S(2)}) collective-permute-start(bf16[2,96,512]{2,1,0:T(8,128)(2,1)S(1)} %pad_maximum_fusion.refs_3_), channel_id=1, source_target_pairs={{0,16},{4,20},{8,24},{12,28},{16,0},{20,4},{24,8},{28,12},{32,48},... | collective-permute-start | bytes 589832 | tf_op jit(solution)/shard_map/ppermute | solution.py:27
  26.1 34.3 %collective-permute-start.8 = (bf16[2,352,512]{2,1,0:T(8,128)(2,1)S(1)}, bf16[2,352,512]{2,1,0:T(8,128)(2,1)S(1)}, u32[]{:S(2)}, u32[]{:S(2)}) collective-permute-start(bf16[2,352,512]{2,1,0:T(8,128)(2,1)S(1)} %shard_map.75.a_ref.refs_6_), channel_id=1, source_target_pairs={{0,4},{4,0},{8,12},{12,8},{16,20},{20,16},{24,28},{28,24},{32,36},... | collective-permute-start | bytes 2162696 | tf_op jit(solution)/shard_map/ppermute | solution.py:27
  32.4 14.7 %collective-permute-start.19 = (bf16[512,512]{1,0:T(8,128)(2,1)S(1)}, bf16[512,512]{1,0:T(8,128)(2,1)S(1)}, u32[]{:S(2)}, u32[]{:S(2)}) collective-permute-start(bf16[512,512]{1,0:T(8,128)(2,1)S(1)} %get-tuple-element.24), channel_id=1, source_target_pairs={{0,1},{1,2},{2,3},{3,0},{4,5},{5,6},{6,7},{7,4},{8,9},{9,10},{10,1... | collective-permute-start | bytes 1572872 | tf_op jit(solution)/shard_map/ppermute | solution.py:32
  33.7 14.3 %collective-permute-start.20 = (bf16[512,512]{1,0:T(8,128)(2,1)S(1)}, bf16[512,512]{1,0:T(8,128)(2,1)S(1)}, u32[]{:S(2)}, u32[]{:S(2)}) collective-permute-start(bf16[512,512]{1,0:T(8,128)(2,1)S(1)} %get-tuple-element.25), channel_id=1, source_target_pairs={{0,3},{1,0},{2,1},{3,2},{4,7},{5,4},{6,5},{7,6},{8,11},{9,8},{10,9... | collective-permute-start | bytes 1572872 | tf_op jit(solution)/shard_map/ppermute | solution.py:32
  35.1 13.7 %collective-permute-start = (bf16[2,256,512]{2,1,0:T(8,128)(2,1)S(1)}, bf16[2,256,512]{2,1,0:T(8,128)(2,1)S(1)}, u32[]{:S(2)}, u32[]{:S(2)}) collective-permute-start(bf16[2,256,512]{2,1,0:T(8,128)(2,1)S(1)} %get-tuple-element.18), channel_id=1, source_target_pairs={{0,4},{4,0},{8,12},{12,8},{16,20},{20,16},{24,28},{28,24},{32,36},... | collective-permute-start | bytes 1572872 | tf_op jit(solution)/shard_map/ppermute | solution.py:27
  35.9 23.5 %collective-permute-start.25 = (bf16[512,512]{1,0:T(8,128)(2,1)S(1)}, bf16[512,512]{1,0:T(8,128)(2,1)S(1)}, u32[]{:S(2)}, u32[]{:S(2)}) collective-permute-start(bf16[512,512]{1,0:T(8,128)(2,1)S(1)} %get-tuple-element.26), channel_id=1, source_target_pairs={{0,2},{1,3},{2,0},{3,1},{4,6},{5,7},{6,4},{7,5},{8,10},{9,11},{10,... | collective-permute-start | bytes 1572872 | tf_op jit(solution)/shard_map/ppermute | solution.py:32
  47.1 24.2 %collective-permute-start.21 = (bf16[512,512]{1,0:T(8,128)(2,1)S(1)}, bf16[512,512]{1,0:T(8,128)(2,1)S(1)}, u32[]{:S(2)}, u32[]{:S(2)}) collective-permute-start(bf16[512,512]{1,0:T(8,128)(2,1)S(1)} %collective-permute-done.19.refs_4_), channel_id=1, source_target_pairs={{0,4},{4,0},{8,12},{12,8},{16,20},{20,16},{24,28},{28,24},{32,36},... | collective-permute-start | bytes 1572872 | tf_op jit(solution)/shard_map/ppermute | solution.py:27
  48.0 23.6 %collective-permute-start.22 = (bf16[512,512]{1,0:T(8,128)(2,1)S(1)}, bf16[512,512]{1,0:T(8,128)(2,1)S(1)}, u32[]{:S(2)}, u32[]{:S(2)}) collective-permute-start(bf16[512,512]{1,0:T(8,128)(2,1)S(1)} %collective-permute-done.20.refs_5_), channel_id=1, source_target_pairs={{0,4},{4,0},{8,12},{12,8},{16,20},{20,16},{24,28},{28,24},{32,36},... | collective-permute-start | bytes 1572872 | tf_op jit(solution)/shard_map/ppermute | solution.py:27
  48.8 16.2 %collective-permute-start.12 = (bf16[2,96,512]{2,1,0:T(8,128)(2,1)S(1)}, bf16[2,96,512]{2,1,0:T(8,128)(2,1)S(1)}, u32[]{:S(2)}, u32[]{:S(2)}) collective-permute-start(bf16[2,96,512]{2,1,0:T(8,128)(2,1)S(1)} %collective-permute-done.9.refs_0_), channel_id=1, source_target_pairs={{0,4},{4,0},{8,12},{12,8},{16,20},{20,16},{24,28},{28,24},{32,36},... | collective-permute-start | bytes 589832 | tf_op jit(solution)/shard_map/ppermute | solution.py:27
  59.4 6.2 %collective-permute-start.13 = (bf16[2,96,512]{2,1,0:T(8,128)(2,1)S(1)}, bf16[2,96,512]{2,1,0:T(8,128)(2,1)S(1)}, u32[]{:S(2)}, u32[]{:S(2)}) collective-permute-start(bf16[2,96,512]{2,1,0:T(8,128)(2,1)S(1)} %collective-permute-done.10.refs_1_), channel_id=1, source_target_pairs={{0,4},{4,0},{8,12},{12,8},{16,20},{20,16},{24,28},{28,24},{32,36},... | collective-permute-start | bytes 589832 | tf_op jit(solution)/shard_map/ppermute | solution.py:27
  65.0 21.6 %collective-permute-start.26 = (bf16[512,512]{1,0:T(8,128)(2,1)S(1)}, bf16[512,512]{1,0:T(8,128)(2,1)S(1)}, u32[]{:S(2)}, u32[]{:S(2)}) collective-permute-start(bf16[512,512]{1,0:T(8,128)(2,1)S(1)} %collective-permute-done.25.refs_2_), channel_id=1, source_target_pairs={{0,4},{4,0},{8,12},{12,8},{16,20},{20,16},{24,28},{28,24},{32,36},... | collective-permute-start | bytes 1572872 | tf_op jit(solution)/shard_map/ppermute | solution.py:27
  67.3 7.9 %collective-permute-start.18 = (bf16[256,512]{1,0:T(8,128)(2,1)S(1)}, bf16[256,512]{1,0:T(8,128)(2,1)S(1)}, u32[]{:S(2)}, u32[]{:S(2)}) collective-permute-start(bf16[256,512]{1,0:T(8,128)(2,1)S(1)} %shard_map.78.b_ref), channel_id=1, source_target_pairs={{0,3},{1,0},{2,1},{3,2},{4,7},{5,4},{6,5},{7,6},{8,11},{9,8},{10,9... | collective-permute-start | bytes 786440 | tf_op jit(solution)/shard_map/ppermute | solution.py:32
  71.2 8.6 %collective-permute-start.15 = (bf16[256,512]{1,0:T(8,128)(2,1)S(1)}, bf16[256,512]{1,0:T(8,128)(2,1)S(1)}, u32[]{:S(2)}, u32[]{:S(2)}) collective-permute-start(bf16[256,512]{1,0:T(8,128)(2,1)S(1)} %shard_map.77.a_ref), channel_id=1, source_target_pairs={{0,1},{1,2},{2,3},{3,0},{4,5},{5,6},{6,7},{7,4},{8,9},{9,10},{10,1... | collective-permute-start | bytes 786440 | tf_op jit(solution)/shard_map/ppermute | solution.py:32
  71.3 14.1 %collective-permute-start.16 = (bf16[256,512]{1,0:T(8,128)(2,1)S(1)}, bf16[256,512]{1,0:T(8,128)(2,1)S(1)}, u32[]{:S(2)}, u32[]{:S(2)}) collective-permute-start(bf16[256,512]{1,0:T(8,128)(2,1)S(1)} %shard_map.78.b_ref), channel_id=1, source_target_pairs={{0,1},{1,2},{2,3},{3,0},{4,5},{5,6},{6,7},{7,4},{8,9},{9,10},{10,1... | collective-permute-start | bytes 786440 | tf_op jit(solution)/shard_map/ppermute | solution.py:32
  71.6 13.8 %collective-permute-start.17 = (bf16[256,512]{1,0:T(8,128)(2,1)S(1)}, bf16[256,512]{1,0:T(8,128)(2,1)S(1)}, u32[]{:S(2)}, u32[]{:S(2)}) collective-permute-start(bf16[256,512]{1,0:T(8,128)(2,1)S(1)} %shard_map.77.a_ref), channel_id=1, source_target_pairs={{0,3},{1,0},{2,1},{3,2},{4,7},{5,4},{6,5},{7,6},{8,11},{9,8},{10,9... | collective-permute-start | bytes 786440 | tf_op jit(solution)/shard_map/ppermute | solution.py:32
  75.3 11.4 %collective-permute-start.24 = (bf16[256,512]{1,0:T(8,128)(2,1)S(1)}, bf16[256,512]{1,0:T(8,128)(2,1)S(1)}, u32[]{:S(2)}, u32[]{:S(2)}) collective-permute-start(bf16[256,512]{1,0:T(8,128)(2,1)S(1)} %collective-permute-done.18.refs_3_), channel_id=1, source_target_pairs={{0,3},{1,0},{2,1},{3,2},{4,7},{5,4},{6,5},{7,6},{8,11},{9,8},{10,9... | collective-permute-start | bytes 786440 | tf_op jit(solution)/shard_map/ppermute | solution.py:32
  79.8 11.2 %collective-permute-start.23 = (bf16[256,512]{1,0:T(8,128)(2,1)S(1)}, bf16[256,512]{1,0:T(8,128)(2,1)S(1)}, u32[]{:S(2)}, u32[]{:S(2)}) collective-permute-start(bf16[256,512]{1,0:T(8,128)(2,1)S(1)} %collective-permute-done.15.refs_0_), channel_id=1, source_target_pairs={{0,1},{1,2},{2,3},{3,0},{4,5},{5,6},{6,7},{7,4},{8,9},{9,10},{10,1... | collective-permute-start | bytes 786440 | tf_op jit(solution)/shard_map/ppermute | solution.py:32
  (7 other events, 247.6 us)
where the time goes:
time: 92.8 us; the launch traced here: 92.7 us
  starting transfers between devices  42.4 us (46%)
  waiting for transfers between devices  34.8 us (37%)
  Pallas kernels  15.3 us (16%)
    ppermute x9, waiting for transfers between devices, turn(): lax.ppermute(block, 'head', [(i, (i + shift) % count) for i in range(coun...  30.4 us
    ppermute x18, starting transfers between devices, flip(): return lax.ppermute(block, 'ctx', [(i, i ^ mask) for i in range(count)])  29.6 us
    ppermute x9, starting transfers between devices, turn(): lax.ppermute(block, 'head', [(i, (i + shift) % count) for i in range(coun...  12.8 us
    ppermute x18, waiting for transfers between devices, flip(): return lax.ppermute(block, 'ctx', [(i, i ^ mask) for i in range(count)])  4.45 us
    pallas_call x2, Pallas kernels, per_device(): call(functools.partial(far_body, block=i, heads=heads), S((rows // 2, wid...  3.42 us
    pallas_call x1, Pallas kernels, per_device(): call(functools.partial(near_body, heads=heads), [S((rows, wide), BF16), S...  2.6 us
    pallas_call x1, Pallas kernels, per_device(): call(functools.partial(prep_body, heads=heads), [S((rows, wide), BF16), S...  2.28 us
    pallas_call x1, Pallas kernels, per_device(): call(functools.partial(mid_body, heads=heads), S((rows, 2 * wide), F32),...  1.99 us
  transfers between devices with their start and end apart: 27, of which 8 were waited for; matrix products, arithmetic and copies ran while one was open for 0% of the time, Pallas kernels for 12%

commit v1 on v0

--- a/solution.py
+++ b/solution.py
@@ -32,12 +32,13 @@
     return lax.ppermute(block, "head", [(i, (i + shift) % count) for i in range(count)])
 
 
-def call(body, outs, specs, scratch=(), flops=0, grant=GRANT):
+def call(body, outs, specs, scratch=(), flops=0, grant=GRANT, place=None, alias=None):
     return pl.pallas_call(
         body,
         out_shape=outs,
         in_specs=specs,
-        out_specs=jax.tree.map(lambda _: VM, outs),
+        out_specs=place or jax.tree.map(lambda _: VM, outs),
+        input_output_aliases=alias or {},
         scratch_shapes=scratch,
         cost_estimate=pl.CostEstimate(flops=flops, bytes_accessed=1 << 20, transcendentals=0),
         compiler_params=pltpu.CompilerParams(vmem_limit_bytes=grant),
@@ -170,24 +171,22 @@
             out_ref[own, wide] = acc_ref[own, wide] + mixin(qs_ref[own, cols], pairs)
 
 
-def far_body(sh_ref, qs_ref, acc_ref, *refs, block, heads):
-    far, both, out_ref = refs[0:6], refs[6:8], refs[8]
+def far_body(sh_ref, qs_ref, acc_ref, *refs, heads):
+    far, outs = refs[0:8], refs[8:10]
     half = qs_ref.shape[0] // 2
-    own = slice(block * half, (block + 1) * half)
     for h in range(heads):
         cols = slice(h * HD, (h + 1) * HD)
         shift = sh_ref[h] * -LOG2E
         pairs = []
         for f in range(3):
-            rows = [
-                jnp.concatenate([gather(far, p, 32 * f, 32, cols), gather(both, p, 256 + 32 * f, 32, cols)], axis=0)
-                for p in range(2)
-            ]
+            rows = [gather(far, p, 32 * f, 32, cols) for p in range(2)]
             pairs.append((rows[0], rows[1], (4.0 + f) * shift))
-        got = mixin(qs_ref[own, cols], pairs)
-        num = acc_ref[own, 2 * h * HD : (2 * h + 1) * HD] + got[:, 0:HD]
-        den = acc_ref[own, (2 * h + 1) * HD : (2 * h + 2) * HD] + got[:, HD:]
-        out_ref[:, cols] = (num / den).astype(BF16)
+        for b in range(2):
+            own = slice(b * half, (b + 1) * half)
+            got = mixin(qs_ref[own, cols], pairs)
+            num = acc_ref[own, 2 * h * HD : (2 * h + 1) * HD] + got[:, 0:HD]
+            den = acc_ref[own, (2 * h + 1) * HD : (2 * h + 2) * HD] + got[:, HD:]
+            outs[b][:, cols] = (num / den).astype(BF16)
 
 
 def own_body(w_ref, a_ref, b_ref, out_ref, buf, sem):
@@ -214,6 +213,23 @@
             for t, w in enumerate(ws):
                 acc += jnp.dot(blocks[2 * t + i][...], w[...], preferred_element_type=F32)
             out_ref[rs, at] = acc.astype(out_ref.dtype)
+
+
+def last_body(*refs, block):
+    acc_ref, a_ref, ours, theirs, out_ref, buf, sem = refs[-7:]
+    width = ours.shape[1]
+    n = a_ref.shape[0]
+    rs = pl.ds(block * n, n)
+    c = lax.axis_index("ctx") % 2
+    copies = []
+    for i, (place, w) in enumerate(((c, ours), (1 - c, theirs))):
+        at = pl.ds(pl.multiple_of(place * width, 128), width)
+        acc = acc_ref[rs, at] + jnp.dot(a_ref[...], w[...], preferred_element_type=F32)
+        buf[i] = acc.astype(BF16)
+        copies.append(pltpu.make_async_copy(buf.at[i], out_ref.at[rs, at], sem.at[i]))
+        copies[-1].start()
+    for copy in copies:
+        copy.wait()
 
 
 def per_device(q, k, v, owner, factor, shift, w):
@@ -267,8 +283,8 @@
     )(owner, factor, shift, q, near, v_in, one_o)
 
     mine = jnp.concatenate([f1[:, 0:32], f2, *f3], axis=1)
-    far_own = [flip(mine, m) for m in (2, 6, 4)]
-    held = call(join_body, S((2, 352, wide), BF16), [VM] * 4)(two_x, three_x2, three_x3, mine)
+    far_own = [mine] + [flip(mine, m) for m in (2, 6, 4)]
+    held = call(join_body, S((2, 256, wide), BF16), [VM] * 3)(two_x, three_x2, three_x3)
     held_o = flip(held, 1)
     acc = call(
         functools.partial(mid_body, heads=heads),
@@ -278,16 +294,12 @@
     )(shift, qs, acc, held, held_o)
 
     far_oth = [flip(b, 1) for b in far_own]
-    att = []
-    for i in range(2):
-        att.append(
-            call(
-                functools.partial(far_body, block=i, heads=heads),
-                S((rows // 2, wide), BF16),
-                [SM] + [VM] * 10,
-                flops=1 << 28,
-            )(shift, qs, acc, *far_own, *far_oth, held, held_o)
-        )
+    att = call(
+        functools.partial(far_body, heads=heads),
+        [S((rows // 2, wide), BF16)] * 2,
+        [SM] + [VM] * 10,
+        flops=1 << 29,
+    )(shift, qs, acc, *far_own, *far_oth)
 
     left = [turn(a, 1) for a in att]
     right = [turn(a, 3) for a in att]
@@ -304,9 +316,20 @@
     out = call(
         functools.partial(add_body, terms=2), S((rows, span), F32), [VM] * 9, flops=1 << 30
     )(out, *left, *right, *send[:2], *w_oth[:2])
-    return call(
-        functools.partial(add_body, terms=1), S((rows, span), BF16), [VM] * 5, flops=1 << 29
-    )(out, *across, send[2], w_oth[2])
+    result = ()
+    for i, a in enumerate(across):
+        result = (
+            call(
+                functools.partial(last_body, block=i),
+                S((rows, span), BF16),
+                [HB] * len(result) + [VM] * 4,
+                scratch=[pltpu.VMEM((2, rows // 2, part), BF16), pltpu.SemaphoreType.DMA((2,))],
+                flops=1 << 28,
+                place=HB,
+                alias={0: 0} if result else None,
+            )(*result, out, a, send[2], w_oth[2]),
+        )
+    return result[0]
 
 
 def solution(mesh):

time: 92.8 us -> 91.5 us (0.986)
  waiting for transfers between devices: 34.8 us -> 22.6 us
  starting transfers between devices: 42.4 us -> 52.9 us
    ppermute x18 -> x19, starting transfers between devices: 29.6 us -> 46.2 us  [flip(): return lax.ppermute(block, 'ctx', [(i, i ^ mask) for i in range(count)])]
    ppermute x9, waiting for transfers between devices: 30.4 us -> 20.1 us  [turn(): lax.ppermute(block, 'head', [(i, (i + shift) % count) for i in range(coun...]
    ppermute x9, starting transfers between devices: 12.8 us -> 6.7 us  [turn(): lax.ppermute(block, 'head', [(i, (i + shift) % count) for i in range(coun...]
    ppermute x18 -> x19, waiting for transfers between devices: 4.45 us -> 2.51 us  [flip(): return lax.ppermute(block, 'ctx', [(i, i ^ mask) for i in range(count)])]
  transfers between devices with their start and end apart: 27 -> 28, of which waited for: 8 -> 9; matrix products, arithmetic and copies ran while one was open for 0% -> 0% of each run, Pallas kernels for 12% -> 13%
where the time goes in v1:
time: 91.5 us; the launch traced here: 91.1 us
  starting transfers between devices  52.9 us (58%)
  waiting for transfers between devices  22.6 us (25%)
  Pallas kernels  15.1 us (17%)
    ppermute x19, starting transfers between devices, flip(): return lax.ppermute(block, 'ctx', [(i, i ^ mask) for i in range(count)])  46.2 us
    ppermute x9, waiting for transfers between devices, turn(): lax.ppermute(block, 'head', [(i, (i + shift) % count) for i in range(coun...  20.1 us
    ppermute x9, starting transfers between devices, turn(): lax.ppermute(block, 'head', [(i, (i + shift) % count) for i in range(coun...  6.7 us
    pallas_call x1, Pallas kernels, per_device(): call(functools.partial(near_body, heads=heads), [S((rows, wide), BF16), S...  2.6 us
    pallas_call x1, Pallas kernels, per_device(): call(functools.partial(far_body, heads=heads), [S((rows // 2, wide), BF16...  2.55 us
    ppermute x19, waiting for transfers between devices, flip(): return lax.ppermute(block, 'ctx', [(i, i ^ mask) for i in range(count)])  2.51 us
    pallas_call x1, Pallas kernels, per_device(): call(functools.partial(prep_body, heads=heads), [S((rows, wide), BF16), S...  2.37 us
    pallas_call x2, Pallas kernels, per_device(): call(functools.partial(last_body, block=i), S((rows, span), BF16), [HB] *...  2.33 us
  transfers between devices with their start and end apart: 28, of which 9 were waited for; matrix products, arithmetic and copies ran while one was open for 0% of the time, Pallas kernels for 13%

profile of v1, /device:TPU:1, one launch (start us, length us, event | category | flops | bytes accessed | tf_op | source)
XLA Modules:
  0.0 91.1 jit_solution(2643864119236114883)
XLA Ops:
  0.0 2.4 %shard_map.73 = (bf16[512,512]{1,0:T(8,128)(2,1)S(1)}, bf16[512,512]{1,0:T(8,128)(2,1)S(1)}, bf16[2,256,512]{2,1,0:T(8,128)(2,1)S(1)}, bf16[2,128,512]{2,1,0:T(8...) custom-call(bf16[512,512]{1,0:T(8,128)(2,1)} %k_hbm.1, ...), custom_call_target="tpu_custom_call" | custom-call | bytes 1048576 | tf_op jit(solution)/shard_map/pallas_call | solution.py:244
  2.4 2.5 %collective-permute-start.5 = (bf16[2,56,512]{2,1,0:T(8,128)(2,1)S(1)}, bf16[2,56,512]{2,1,0:T(8,128)(2,1)S(1)}, u32[]{:S(2)}, u32[]{:S(2)}) collective-permute-start(bf16[2,56,512]{2,1,0:T(8,128)(2,1)S(1)} %get-tuple-element.25), channel_id=1, source_target_pairs={{0,32},{4,36},{8,40},{12,44},{16,48},{20,52},{24,56},{28,60},{32,0... | collective-permute-start | bytes 344072 | tf_op jit(solution)/shard_map/ppermute | solution.py:27
  6.2 2.5 %collective-permute-start.2 = (bf16[2,64,512]{2,1,0:T(8,128)(2,1)S(1)}, bf16[2,64,512]{2,1,0:T(8,128)(2,1)S(1)}, u32[]{:S(2)}, u32[]{:S(2)}) collective-permute-start(bf16[2,64,512]{2,1,0:T(8,128)(2,1)S(1)} %get-tuple-element.24), channel_id=1, source_target_pairs={{0,16},{4,20},{8,24},{12,28},{16,0},{20,4},{24,8},{28,12},{32,48},... | collective-permute-start | bytes 393224 | tf_op jit(solution)/shard_map/ppermute | solution.py:27
  8.8 3.1 %collective-permute-start.6 = (bf16[2,32,512]{2,1,0:T(8,128)(2,1)S(1)}, bf16[2,32,512]{2,1,0:T(8,128)(2,1)S(1)}, u32[]{:S(2)}, u32[]{:S(2)}) collective-permute-start(bf16[2,32,512]{2,1,0:T(8,128)(2,1)S(1)} %pad_maximum_fusion.1), channel_id=1, source_target_pairs={{0,64},{4,68},{8,72},{12,76},{16,80},{20,84},{24,88},{28,92},{32,9... | collective-permute-start | bytes 196616 | tf_op jit(solution)/shard_map/ppermute | solution.py:27
  11.9 3.8 %collective-permute-start.7 = (bf16[2,16,512]{2,1,0:T(8,128)(2,1)S(1)}, bf16[2,16,512]{2,1,0:T(8,128)(2,1)S(1)}, u32[]{:S(2)}, u32[]{:S(2)}) collective-permute-start(bf16[2,16,512]{2,1,0:T(8,128)(2,1)S(1)} %pad_maximum_fusion.2), channel_id=1, source_target_pairs={{0,160},{4,164},{8,168},{12,172},{16,176},{20,180},{24,184},{28,18... | collective-permute-start | bytes 98312 | tf_op jit(solution)/shard_map/ppermute | solution.py:27
  16.6 5.1 %collective-permute-start.8 = (bf16[2,16,512]{2,1,0:T(8,128)(2,1)S(1)}, bf16[2,16,512]{2,1,0:T(8,128)(2,1)S(1)}, u32[]{:S(2)}, u32[]{:S(2)}) collective-permute-start(bf16[2,16,512]{2,1,0:T(8,128)(2,1)S(1)} %pad_maximum_fusion.2), channel_id=1, source_target_pairs={{0,192},{4,196},{8,200},{12,204},{16,208},{20,212},{24,216},{28,22... | collective-permute-start | bytes 98312 | tf_op jit(solution)/shard_map/ppermute | solution.py:27
  21.7 2.6 %collective-permute-start = (bf16[2,256,512]{2,1,0:T(8,128)(2,1)S(1)}, bf16[2,256,512]{2,1,0:T(8,128)(2,1)S(1)}, u32[]{:S(2)}, u32[]{:S(2)}) collective-permute-start(bf16[2,256,512]{2,1,0:T(8,128)(2,1)S(1)} %get-tuple-element.20), channel_id=1, source_target_pairs={{0,4},{4,0},{8,12},{12,8},{16,20},{20,16},{24,28},{28,24},{32,36},... | collective-permute-start | bytes 1572872 | tf_op jit(solution)/shard_map/ppermute | solution.py:27
  25.3 2.5 %collective-permute-start.11 = (bf16[2,96,512]{2,1,0:T(8,128)(2,1)S(1)}, bf16[2,96,512]{2,1,0:T(8,128)(2,1)S(1)}, u32[]{:S(2)}, u32[]{:S(2)}) collective-permute-start(bf16[2,96,512]{2,1,0:T(8,128)(2,1)S(1)} %pad_maximum_fusion.refs_0_), channel_id=1, source_target_pairs={{0,16},{4,20},{8,24},{12,28},{16,0},{20,4},{24,8},{28,12},{32,48},... | collective-permute-start | bytes 589832 | tf_op jit(solution)/shard_map/ppermute | solution.py:27
  27.8 1.6 %collective-permute-done.9.refs_1_ = bf16[2,96,512]{2,1,0:T(8,128)(2,1)S(1)} collective-permute-done((bf16[2,96,512]{2,1,0:T(8,128)(2,1)S(1)}, bf16[2,96,512]{2,1,0:T(8,128)(2,1)S(1)}, u32[]{:S(2)}, u32[]{:S(2)}) %collective-permute-start.9) | collective-permute-done | bytes 196640 | tf_op jit(solution)/shard_map/ppermute | solution.py:27
  29.4 4.5 %collective-permute-start.12 = (bf16[2,96,512]{2,1,0:T(8,128)(2,1)S(1)}, bf16[2,96,512]{2,1,0:T(8,128)(2,1)S(1)}, u32[]{:S(2)}, u32[]{:S(2)}) collective-permute-start(bf16[2,96,512]{2,1,0:T(8,128)(2,1)S(1)} %pad_maximum_fusion.refs_0_), channel_id=1, source_target_pairs={{0,4},{4,0},{8,12},{12,8},{16,20},{20,16},{24,28},{28,24},{32,36},... | collective-permute-start | bytes 589832 | tf_op jit(solution)/shard_map/ppermute | solution.py:27
  33.9 3.4 %collective-permute-start.13 = (bf16[2,96,512]{2,1,0:T(8,128)(2,1)S(1)}, bf16[2,96,512]{2,1,0:T(8,128)(2,1)S(1)}, u32[]{:S(2)}, u32[]{:S(2)}) collective-permute-start(bf16[2,96,512]{2,1,0:T(8,128)(2,1)S(1)} %collective-permute-done.9.refs_1_), channel_id=1, source_target_pairs={{0,4},{4,0},{8,12},{12,8},{16,20},{20,16},{24,28},{28,24},{32,36},... | collective-permute-start | bytes 589832 | tf_op jit(solution)/shard_map/ppermute | solution.py:27
  37.4 1.3 %collective-permute-start.20 = (bf16[512,512]{1,0:T(8,128)(2,1)S(1)}, bf16[512,512]{1,0:T(8,128)(2,1)S(1)}, u32[]{:S(2)}, u32[]{:S(2)}) collective-permute-start(bf16[512,512]{1,0:T(8,128)(2,1)S(1)} %get-tuple-element.28), channel_id=1, source_target_pairs={{0,1},{1,2},{2,3},{3,0},{4,5},{5,6},{6,7},{7,4},{8,9},{9,10},{10,1... | collective-permute-start | bytes 1572872 | tf_op jit(solution)/shard_map/ppermute | solution.py:32
  38.7 1.5 %collective-permute-start.21 = (bf16[512,512]{1,0:T(8,128)(2,1)S(1)}, bf16[512,512]{1,0:T(8,128)(2,1)S(1)}, u32[]{:S(2)}, u32[]{:S(2)}) collective-permute-start(bf16[512,512]{1,0:T(8,128)(2,1)S(1)} %get-tuple-element.29), channel_id=1, source_target_pairs={{0,3},{1,0},{2,1},{3,2},{4,7},{5,4},{6,5},{7,6},{8,11},{9,8},{10,9... | collective-permute-start | bytes 1572872 | tf_op jit(solution)/shard_map/ppermute | solution.py:32
  40.2 1.6 %collective-permute-start.25 = (bf16[512,512]{1,0:T(8,128)(2,1)S(1)}, bf16[512,512]{1,0:T(8,128)(2,1)S(1)}, u32[]{:S(2)}, u32[]{:S(2)}) collective-permute-start(bf16[512,512]{1,0:T(8,128)(2,1)S(1)} %get-tuple-element.30), channel_id=1, source_target_pairs={{0,2},{1,3},{2,0},{3,1},{4,6},{5,7},{6,4},{7,5},{8,10},{9,11},{10,... | collective-permute-start | bytes 1572872 | tf_op jit(solution)/shard_map/ppermute | solution.py:32
  42.9 2.6 %shard_map.74 = (bf16[512,512]{1,0:T(8,128)(2,1)S(1)}, f32[512,1024]{1,0:T(8,128)S(1)}) custom-call(s32[2]{0:T(128)S(1)} %copy-done.2, f32[4]{0:T(128)S(1)} %copy-done.3, f32[4]{0:T(128)S(1)} %copy-done, bf16[512,512]{1,0:T(8,128)(2,1)S(1)} %copy-done.1, bf16[512,512]{1,0:T(8,128)(2,1)S(1)} %get-tuple-element.18.near_ref, ...), custom_call_target="tpu_custom_call" | custom-call | flops 1073741824 | bytes 1048576 | tf_op jit(solution)/shard_map/pallas_call | solution.py:278
  45.5 2.0 %shard_map.76.acc_ref = f32[512,1024]{1,0:T(8,128)S(1)} custom-call(f32[4]{0:T(128)S(1)} %copy-done, bf16[512,512]{1,0:T(8,128)(2,1)S(1)} %get-tuple-element.21.qs_ref, f32[512,1024]{1,0:T(8,128)S(1)} %get-tuple-element.22.acc_ref, bf16[2,256,512]{2,1,0:T(8,128)(2,1)S(1)} %shard_map.75.a_ref, bf16[2,256,512]{2,1,0:T(8,128)(2,1)S(1)} %collective-permute-done.4.b_ref), custom_call_target="tpu_custom_call" | custom-call | flops 536870912 | bytes 1048576 | tf_op jit(solution)/shard_map/pallas_call | solution.py:289
  47.5 2.5 %shard_map.77 = (bf16[256,512]{1,0:T(8,128)(2,1)S(1)}, bf16[256,512]{1,0:T(8,128)(2,1)S(1)}) custom-call(f32[4]{0:T(128)S(1)} %copy-done, bf16[512,512]{1,0:T(8,128)(2,1)S(1)} %get-tuple-element.21.qs_ref, f32[512,1024]{1,0:T(8,128)S(1)} %shard_map.76.acc_ref, bf16[2,96,512]{2,1,0:T(8,128)(2,1)S(1)} %pad_maximum_fusion.refs_0_, ...), custom_call_target="tpu_custom_call" | custom-call | flops 536870912 | bytes 1048576 | tf_op jit(solution)/shard_map/pallas_call | solution.py:297
  53.0 10.6 %collective-permute-start.23 = (bf16[512,512]{1,0:T(8,128)(2,1)S(1)}, bf16[512,512]{1,0:T(8,128)(2,1)S(1)}, u32[]{:S(2)}, u32[]{:S(2)}) collective-permute-start(bf16[512,512]{1,0:T(8,128)(2,1)S(1)} %collective-permute-done.21.refs_5_), channel_id=1, source_target_pairs={{0,4},{4,0},{8,12},{12,8},{16,20},{20,16},{24,28},{28,24},{32,36},... | collective-permute-start | bytes 1572872 | tf_op jit(solution)/shard_map/ppermute | solution.py:27
  64.6 1.3 %collective-permute-start.26 = (bf16[512,512]{1,0:T(8,128)(2,1)S(1)}, bf16[512,512]{1,0:T(8,128)(2,1)S(1)}, u32[]{:S(2)}, u32[]{:S(2)}) collective-permute-start(bf16[512,512]{1,0:T(8,128)(2,1)S(1)} %collective-permute-done.25.refs_2_.refs_3_), channel_id=1, source_target_pairs={{0,4},{4,0},{8,12},{12,8},{16,20},{20,16},{24,28},{28,24},{32,36},... | collective-permute-start | bytes 1572872 | tf_op jit(solution)/shard_map/ppermute | solution.py:27
  65.9 4.5 %collective-permute-done.16.refs_0_ = bf16[256,512]{1,0:T(8,128)(2,1)S(1)} collective-permute-done((bf16[256,512]{1,0:T(8,128)(2,1)S(1)}, bf16[256,512]{1,0:T(8,128)(2,1)S(1)}, u32[]{:S(2)}, u32[]{:S(2)}) %collective-permute-start.16) | collective-permute-done | bytes 262176 | tf_op jit(solution)/shard_map/ppermute | solution.py:32
  70.5 5.5 %collective-permute-done.17.refs_1_ = bf16[256,512]{1,0:T(8,128)(2,1)S(1)} collective-permute-done((bf16[256,512]{1,0:T(8,128)(2,1)S(1)}, bf16[256,512]{1,0:T(8,128)(2,1)S(1)}, u32[]{:S(2)}, u32[]{:S(2)}) %collective-permute-start.17) | collective-permute-done | bytes 262176 | tf_op jit(solution)/shard_map/ppermute | solution.py:32
  76.1 1.4 %collective-permute-done.18.refs_2_ = bf16[256,512]{1,0:T(8,128)(2,1)S(1)} collective-permute-done((bf16[256,512]{1,0:T(8,128)(2,1)S(1)}, bf16[256,512]{1,0:T(8,128)(2,1)S(1)}, u32[]{:S(2)}, u32[]{:S(2)}) %collective-permute-start.18) | collective-permute-done | bytes 262176 | tf_op jit(solution)/shard_map/ppermute | solution.py:32
  77.5 5.8 %collective-permute-done.19.refs_3_ = bf16[256,512]{1,0:T(8,128)(2,1)S(1)} collective-permute-done((bf16[256,512]{1,0:T(8,128)(2,1)S(1)}, bf16[256,512]{1,0:T(8,128)(2,1)S(1)}, u32[]{:S(2)}, u32[]{:S(2)}) %collective-permute-start.19) | collective-permute-done | bytes 262176 | tf_op jit(solution)/shard_map/ppermute | solution.py:32
  84.3 2.0 %shard_map.78.acc_ref = f32[512,1024]{1,0:T(8,128)S(1)} custom-call(bf16[512,4096]{1,0:T(8,128)(2,1)} %w_ref.1, bf16[256,512]{1,0:T(8,128)(2,1)S(1)} %get-tuple-element.26.a_ref, bf16[256,512]{1,0:T(8,128)(2,1)S(1)} %get-tuple-element.27.b_ref), custom_call_target="tpu_custom_call" | custom-call | flops 536870912 | bytes 1048576 | tf_op jit(solution)/shard_map/pallas_call | solution.py:309
  (57 shorter events, 14.2 us)
Async XLA Ops:
  4.9 19.3 %collective-permute-start.1 = (bf16[2,128,512]{2,1,0:T(8,128)(2,1)S(1)}, bf16[2,128,512]{2,1,0:T(8,128)(2,1)S(1)}, u32[]{:S(2)}, u32[]{:S(2)}) collective-permute-start(bf16[2,128,512]{2,1,0:T(8,128)(2,1)S(1)} %get-tuple-element.23), channel_id=1, source_target_pairs={{0,8},{4,12},{8,0},{12,4},{16,24},{20,28},{24,16},{28,20},{32,40},... | collective-permute-start | bytes 786440 | tf_op jit(solution)/shard_map/ppermute | solution.py:27
  6.2 10.4 %collective-permute-start.2 = (bf16[2,64,512]{2,1,0:T(8,128)(2,1)S(1)}, bf16[2,64,512]{2,1,0:T(8,128)(2,1)S(1)}, u32[]{:S(2)}, u32[]{:S(2)}) collective-permute-start(bf16[2,64,512]{2,1,0:T(8,128)(2,1)S(1)} %get-tuple-element.24), channel_id=1, source_target_pairs={{0,16},{4,20},{8,24},{12,28},{16,0},{20,4},{24,8},{28,12},{32,48},... | collective-permute-start | bytes 393224 | tf_op jit(solution)/shard_map/ppermute | solution.py:27
  8.6 13.1 %collective-permute-start.3 = (bf16[2,64,512]{2,1,0:T(8,128)(2,1)S(1)}, bf16[2,64,512]{2,1,0:T(8,128)(2,1)S(1)}, u32[]{:S(2)}, u32[]{:S(2)}) collective-permute-start(bf16[2,64,512]{2,1,0:T(8,128)(2,1)S(1)} %get-tuple-element.24), channel_id=1, source_target_pairs={{0,24},{4,28},{8,16},{12,20},{16,8},{20,12},{24,0},{28,4},{32,56},... | collective-permute-start | bytes 393224 | tf_op jit(solution)/shard_map/ppermute | solution.py:27
  8.8 15.6 %collective-permute-start.6 = (bf16[2,32,512]{2,1,0:T(8,128)(2,1)S(1)}, bf16[2,32,512]{2,1,0:T(8,128)(2,1)S(1)}, u32[]{:S(2)}, u32[]{:S(2)}) collective-permute-start(bf16[2,32,512]{2,1,0:T(8,128)(2,1)S(1)} %pad_maximum_fusion.1), channel_id=1, source_target_pairs={{0,64},{4,68},{8,72},{12,76},{16,80},{20,84},{24,88},{28,92},{32,9... | collective-permute-start | bytes 196616 | tf_op jit(solution)/shard_map/ppermute | solution.py:27
  11.9 12.5 %collective-permute-start.7 = (bf16[2,16,512]{2,1,0:T(8,128)(2,1)S(1)}, bf16[2,16,512]{2,1,0:T(8,128)(2,1)S(1)}, u32[]{:S(2)}, u32[]{:S(2)}) collective-permute-start(bf16[2,16,512]{2,1,0:T(8,128)(2,1)S(1)} %pad_maximum_fusion.2), channel_id=1, source_target_pairs={{0,160},{4,164},{8,168},{12,172},{16,176},{20,180},{24,184},{28,18... | collective-permute-start | bytes 98312 | tf_op jit(solution)/shard_map/ppermute | solution.py:27
  16.6 7.9 %collective-permute-start.8 = (bf16[2,16,512]{2,1,0:T(8,128)(2,1)S(1)}, bf16[2,16,512]{2,1,0:T(8,128)(2,1)S(1)}, u32[]{:S(2)}, u32[]{:S(2)}) collective-permute-start(bf16[2,16,512]{2,1,0:T(8,128)(2,1)S(1)} %pad_maximum_fusion.2), channel_id=1, source_target_pairs={{0,192},{4,196},{8,200},{12,204},{16,208},{20,212},{24,216},{28,22... | collective-permute-start | bytes 98312 | tf_op jit(solution)/shard_map/ppermute | solution.py:27
  21.7 18.5 %collective-permute-start = (bf16[2,256,512]{2,1,0:T(8,128)(2,1)S(1)}, bf16[2,256,512]{2,1,0:T(8,128)(2,1)S(1)}, u32[]{:S(2)}, u32[]{:S(2)}) collective-permute-start(bf16[2,256,512]{2,1,0:T(8,128)(2,1)S(1)} %get-tuple-element.20), channel_id=1, source_target_pairs={{0,4},{4,0},{8,12},{12,8},{16,20},{20,16},{24,28},{28,24},{32,36},... | collective-permute-start | bytes 1572872 | tf_op jit(solution)/shard_map/ppermute | solution.py:27
  24.3 18.3 %collective-permute-start.4 = (bf16[2,256,512]{2,1,0:T(8,128)(2,1)S(1)}, bf16[2,256,512]{2,1,0:T(8,128)(2,1)S(1)}, u32[]{:S(2)}, u32[]{:S(2)}) collective-permute-start(bf16[2,256,512]{2,1,0:T(8,128)(2,1)S(1)} %shard_map.75.a_ref), channel_id=1, source_target_pairs={{0,4},{4,0},{8,12},{12,8},{16,20},{20,16},{24,28},{28,24},{32,36},... | collective-permute-start | bytes 1572872 | tf_op jit(solution)/shard_map/ppermute | solution.py:27
  24.6 9.4 %collective-permute-start.10 = (bf16[2,96,512]{2,1,0:T(8,128)(2,1)S(1)}, bf16[2,96,512]{2,1,0:T(8,128)(2,1)S(1)}, u32[]{:S(2)}, u32[]{:S(2)}) collective-permute-start(bf16[2,96,512]{2,1,0:T(8,128)(2,1)S(1)} %pad_maximum_fusion.refs_0_), channel_id=1, source_target_pairs={{0,24},{4,28},{8,16},{12,20},{16,8},{20,12},{24,0},{28,4},{32,56},... | collective-permute-start | bytes 589832 | tf_op jit(solution)/shard_map/ppermute | solution.py:27
  25.3 12.1 %collective-permute-start.11 = (bf16[2,96,512]{2,1,0:T(8,128)(2,1)S(1)}, bf16[2,96,512]{2,1,0:T(8,128)(2,1)S(1)}, u32[]{:S(2)}, u32[]{:S(2)}) collective-permute-start(bf16[2,96,512]{2,1,0:T(8,128)(2,1)S(1)} %pad_maximum_fusion.refs_0_), channel_id=1, source_target_pairs={{0,16},{4,20},{8,24},{12,28},{16,0},{20,4},{24,8},{28,12},{32,48},... | collective-permute-start | bytes 589832 | tf_op jit(solution)/shard_map/ppermute | solution.py:27
  29.4 9.3 %collective-permute-start.12 = (bf16[2,96,512]{2,1,0:T(8,128)(2,1)S(1)}, bf16[2,96,512]{2,1,0:T(8,128)(2,1)S(1)}, u32[]{:S(2)}, u32[]{:S(2)}) collective-permute-start(bf16[2,96,512]{2,1,0:T(8,128)(2,1)S(1)} %pad_maximum_fusion.refs_0_), channel_id=1, source_target_pairs={{0,4},{4,0},{8,12},{12,8},{16,20},{20,16},{24,28},{28,24},{32,36},... | collective-permute-start | bytes 589832 | tf_op jit(solution)/shard_map/ppermute | solution.py:27
  33.9 7.8 %collective-permute-start.13 = (bf16[2,96,512]{2,1,0:T(8,128)(2,1)S(1)}, bf16[2,96,512]{2,1,0:T(8,128)(2,1)S(1)}, u32[]{:S(2)}, u32[]{:S(2)}) collective-permute-start(bf16[2,96,512]{2,1,0:T(8,128)(2,1)S(1)} %collective-permute-done.9.refs_1_), channel_id=1, source_target_pairs={{0,4},{4,0},{8,12},{12,8},{16,20},{20,16},{24,28},{28,24},{32,36},... | collective-permute-start | bytes 589832 | tf_op jit(solution)/shard_map/ppermute | solution.py:27
  37.4 14.8 %collective-permute-start.20 = (bf16[512,512]{1,0:T(8,128)(2,1)S(1)}, bf16[512,512]{1,0:T(8,128)(2,1)S(1)}, u32[]{:S(2)}, u32[]{:S(2)}) collective-permute-start(bf16[512,512]{1,0:T(8,128)(2,1)S(1)} %get-tuple-element.28), channel_id=1, source_target_pairs={{0,1},{1,2},{2,3},{3,0},{4,5},{5,6},{6,7},{7,4},{8,9},{9,10},{10,1... | collective-permute-start | bytes 1572872 | tf_op jit(solution)/shard_map/ppermute | solution.py:32
  38.7 14.3 %collective-permute-start.21 = (bf16[512,512]{1,0:T(8,128)(2,1)S(1)}, bf16[512,512]{1,0:T(8,128)(2,1)S(1)}, u32[]{:S(2)}, u32[]{:S(2)}) collective-permute-start(bf16[512,512]{1,0:T(8,128)(2,1)S(1)} %get-tuple-element.29), channel_id=1, source_target_pairs={{0,3},{1,0},{2,1},{3,2},{4,7},{5,4},{6,5},{7,6},{8,11},{9,8},{10,9... | collective-permute-start | bytes 1572872 | tf_op jit(solution)/shard_map/ppermute | solution.py:32
  40.2 24.4 %collective-permute-start.25 = (bf16[512,512]{1,0:T(8,128)(2,1)S(1)}, bf16[512,512]{1,0:T(8,128)(2,1)S(1)}, u32[]{:S(2)}, u32[]{:S(2)}) collective-permute-start(bf16[512,512]{1,0:T(8,128)(2,1)S(1)} %get-tuple-element.30), channel_id=1, source_target_pairs={{0,2},{1,3},{2,0},{3,1},{4,6},{5,7},{6,4},{7,5},{8,10},{9,11},{10,... | collective-permute-start | bytes 1572872 | tf_op jit(solution)/shard_map/ppermute | solution.py:32
  50.1 20.3 %collective-permute-start.16 = (bf16[256,512]{1,0:T(8,128)(2,1)S(1)}, bf16[256,512]{1,0:T(8,128)(2,1)S(1)}, u32[]{:S(2)}, u32[]{:S(2)}) collective-permute-start(bf16[256,512]{1,0:T(8,128)(2,1)S(1)} %get-tuple-element.26.a_ref), channel_id=1, source_target_pairs={{0,1},{1,2},{2,3},{3,0},{4,5},{5,6},{6,7},{7,4},{8,9},{9,10},{10,1... | collective-permute-start | bytes 786440 | tf_op jit(solution)/shard_map/ppermute | solution.py:32
  50.6 25.4 %collective-permute-start.17 = (bf16[256,512]{1,0:T(8,128)(2,1)S(1)}, bf16[256,512]{1,0:T(8,128)(2,1)S(1)}, u32[]{:S(2)}, u32[]{:S(2)}) collective-permute-start(bf16[256,512]{1,0:T(8,128)(2,1)S(1)} %get-tuple-element.27.b_ref), channel_id=1, source_target_pairs={{0,1},{1,2},{2,3},{3,0},{4,5},{5,6},{6,7},{7,4},{8,9},{9,10},{10,1... | collective-permute-start | bytes 786440 | tf_op jit(solution)/shard_map/ppermute | solution.py:32
  52.2 34.1 %collective-permute-start.22 = (bf16[512,512]{1,0:T(8,128)(2,1)S(1)}, bf16[512,512]{1,0:T(8,128)(2,1)S(1)}, u32[]{:S(2)}, u32[]{:S(2)}) collective-permute-start(bf16[512,512]{1,0:T(8,128)(2,1)S(1)} %collective-permute-done.20.refs_4_), channel_id=1, source_target_pairs={{0,4},{4,0},{8,12},{12,8},{16,20},{20,16},{24,28},{28,24},{32,36},... | collective-permute-start | bytes 1572872 | tf_op jit(solution)/shard_map/ppermute | solution.py:27
  53.0 33.3 %collective-permute-start.23 = (bf16[512,512]{1,0:T(8,128)(2,1)S(1)}, bf16[512,512]{1,0:T(8,128)(2,1)S(1)}, u32[]{:S(2)}, u32[]{:S(2)}) collective-permute-start(bf16[512,512]{1,0:T(8,128)(2,1)S(1)} %collective-permute-done.21.refs_5_), channel_id=1, source_target_pairs={{0,4},{4,0},{8,12},{12,8},{16,20},{20,16},{24,28},{28,24},{32,36},... | collective-permute-start | bytes 1572872 | tf_op jit(solution)/shard_map/ppermute | solution.py:27
  64.6 23.0 %collective-permute-start.26 = (bf16[512,512]{1,0:T(8,128)(2,1)S(1)}, bf16[512,512]{1,0:T(8,128)(2,1)S(1)}, u32[]{:S(2)}, u32[]{:S(2)}) collective-permute-start(bf16[512,512]{1,0:T(8,128)(2,1)S(1)} %collective-permute-done.25.refs_2_.refs_3_), channel_id=1, source_target_pairs={{0,4},{4,0},{8,12},{12,8},{16,20},{20,16},{24,28},{28,24},{32,36},... | collective-permute-start | bytes 1572872 | tf_op jit(solution)/shard_map/ppermute | solution.py:27
  70.4 7.1 %collective-permute-start.18 = (bf16[256,512]{1,0:T(8,128)(2,1)S(1)}, bf16[256,512]{1,0:T(8,128)(2,1)S(1)}, u32[]{:S(2)}, u32[]{:S(2)}) collective-permute-start(bf16[256,512]{1,0:T(8,128)(2,1)S(1)} %get-tuple-element.26.a_ref), channel_id=1, source_target_pairs={{0,3},{1,0},{2,1},{3,2},{4,7},{5,4},{6,5},{7,6},{8,11},{9,8},{10,9... | collective-permute-start | bytes 786440 | tf_op jit(solution)/shard_map/ppermute | solution.py:32
  76.0 7.3 %collective-permute-start.19 = (bf16[256,512]{1,0:T(8,128)(2,1)S(1)}, bf16[256,512]{1,0:T(8,128)(2,1)S(1)}, u32[]{:S(2)}, u32[]{:S(2)}) collective-permute-start(bf16[256,512]{1,0:T(8,128)(2,1)S(1)} %get-tuple-element.27.b_ref), channel_id=1, source_target_pairs={{0,3},{1,0},{2,1},{3,2},{4,7},{5,4},{6,5},{7,6},{8,11},{9,8},{10,9... | collective-permute-start | bytes 786440 | tf_op jit(solution)/shard_map/ppermute | solution.py:32
  77.5 10.1 %collective-permute-start.24 = (bf16[256,512]{1,0:T(8,128)(2,1)S(1)}, bf16[256,512]{1,0:T(8,128)(2,1)S(1)}, u32[]{:S(2)}, u32[]{:S(2)}) collective-permute-start(bf16[256,512]{1,0:T(8,128)(2,1)S(1)} %collective-permute-done.16.refs_0_), channel_id=1, source_target_pairs={{0,1},{1,2},{2,3},{3,0},{4,5},{5,6},{6,7},{7,4},{8,9},{9,10},{10,1... | collective-permute-start | bytes 786440 | tf_op jit(solution)/shard_map/ppermute | solution.py:32
  83.3 6.4 %collective-permute-start.27 = (bf16[256,512]{1,0:T(8,128)(2,1)S(1)}, bf16[256,512]{1,0:T(8,128)(2,1)S(1)}, u32[]{:S(2)}, u32[]{:S(2)}) collective-permute-start(bf16[256,512]{1,0:T(8,128)(2,1)S(1)} %collective-permute-done.19.refs_3_), channel_id=1, source_target_pairs={{0,3},{1,0},{2,1},{3,2},{4,7},{5,4},{6,5},{7,6},{8,11},{9,8},{10,9... | collective-permute-start | bytes 786440 | tf_op jit(solution)/shard_map/ppermute | solution.py:32
  (8 other events, 193.6 us)
